TPU v7x, 128 devices: a whole 4x4x4 slice. The times are simulated.
128 devices in a mesh: grp: 4 (over x), mem: 32 (over z, y, core).
Axes of the slice: x: 4, y: 4, z: 4, core: 2. Of those that a mesh axis runs over, the one named last changes fastest.
Arguments:
- embeddings: bfloat16 [16384, 1024], P(('grp', 'mem')), may hold values from -6 to 6
- cluster: int32 [16384, 1], P(('grp', 'mem')), may hold values from 0 to 3; in each aligned block of 128 rows (0 to 127, 128 to 255, ...) at most 64 rows name the same one
- rank: int32 [16384], P(('grp', 'mem')), may hold values from 0 to 1048575
Outputs:
- similarity: float32 [16384], P(('grp', 'mem'))
Inputs may be any that keep to these rules, and one draw needn't show every extreme that they name: `cluster`: in each aligned block of 128 rows (the rows of one device) no group is named by more than 64 rows. A smaller rank is earlier; equal ranks are not earlier.
All inputs are finite; a program needn't handle non-finite values.
Results may differ from a plain program's by a relative error of at most 0.0013.
Values may be sent and summed in bfloat16 or wider, within the bound.
A program may use at most 64 MiB of HBM per device.

v0:
```python
import jax
import jax.numpy as jnp
from jax import lax
from jax.sharding import PartitionSpec as P

absent_rank = 1073741824


def block_gram(queries, others):
    return lax.dot_general(
        queries, others, (((1,), (1,)), ((), ())), preferred_element_type=jnp.float32
    )


def row_maxima(gram, query_rank, other_rank):
    earlier = other_rank[None, :] < query_rank[:, None]
    return jnp.max(jnp.where(earlier, gram, jnp.float32(-1.0)), axis=1)


def body(embeddings, cluster, rank):
    rows = embeddings.shape[0]
    width = embeddings.shape[1]
    groups = lax.axis_size("grp")
    capacity = max(2, 2 * rows // groups)
    slots = groups * capacity
    wide = embeddings.astype(jnp.float32)
    normed = (wide * lax.rsqrt(jnp.sum(wide * wide, axis=1, keepdims=True) + 1e-06)).astype(
        jnp.bfloat16
    )
    owner = cluster[:, 0]
    onehot = (owner[:, None] == jnp.arange(groups, dtype=jnp.int32)[None, :]).astype(jnp.int32)
    before = jnp.cumsum(onehot, axis=0) - onehot
    position = jnp.sum(before * onehot, axis=1)
    slot = owner * capacity + position
    outgoing = jnp.zeros((slots, width), jnp.bfloat16).at[slot].set(normed)
    out_rank = jnp.full((slots,), absent_rank, jnp.int32).at[slot].set(rank)
    keys, key_rank = (
        lax.all_to_all(outgoing, "grp", split_axis=0, concat_axis=0, tiled=True),
        lax.all_to_all(out_rank, "grp", split_axis=0, concat_axis=0, tiled=True),
    )
    gram = block_gram(keys, lax.all_gather(keys, "mem", axis=0, tiled=True))
    best = jnp.maximum(
        jnp.full((slots,), -1.0, jnp.float32),
        row_maxima(gram, key_rank, lax.all_gather(key_rank, "mem", axis=0, tiled=True)),
    )
    home = lax.all_to_all(best, "grp", split_axis=0, concat_axis=0, tiled=True)
    return home[slot]


def solution(mesh):
    in_specs = (P(("grp", "mem"), None), P(("grp", "mem"), None), P(("grp", "mem")))
    out_specs = P(("grp", "mem"))
    return jax.shard_map(body, mesh=mesh, in_specs=in_specs, out_specs=out_specs, check_vma=False)
```

profile of v0, /device:TPU:0, one launch (start us, length us, event | category | flops | bytes accessed | tf_op | source)
XLA Modules:
  0.0 129.6 jit_solution(2143554724468487378)
XLA Ops:
  6.5 0.0 all-gather.3.cloned.1.call-start
  6.5 0.7 fusion.7
  7.3 0.2 reduce_window_sum.11
  7.5 0.8 select_reduce_fusion
  8.3 0.7 fusion.8
  9.0 1.1 fusion.1
  10.0 1.8 %scatter_custom_fusion.1 = bf16[256,1024]{1,0:T(8,128)(2,1)S(1)} fusion(s32[128]{0:T(128)S(1)} %fusion.8, bf16[128,1024]{1,0:T(8,128)(2,1)} %param.3, f32[128]{0:T(128)S(1)} %add_rsqrt_fusion, bf16[]{:T(256)} %constant.4.clone.1), kind=kCustom, calls=%fused_computation.9 | custom fusion | flops 393216 | bytes 786946 | tf_op jit(solution)/shard_map/scatter | solution.py:35
  11.8 13.8 %all_to_all.33 = bf16[4,64,1024]{2,1,0:T(8,128)(2,1)} all-to-all(bf16[4,64,1024]{2,1,0:T(8,128)(2,1)S(1)} %bitcast.19), channel_id=1, replica_groups=mesh['grp'=4,'mem'=32] {'grp'}, dimensions={0} | all-to-all | bytes 1048576 | tf_op jit(solution)/shard_map/all_to_all | solution.py:38
  25.6 0.0 all-gather.3.cloned.1.call-update
  25.7 1.1 scatter_custom_fusion
  26.8 0.1 all_to_all.22
  26.9 7.6 %all_to_all.34 = s32[4,64,1]{1,2,0:T(1,128)S(1)} all-to-all(s32[4,64,1]{1,2,0:T(1,128)S(1)} %bitcast.22), channel_id=1, replica_groups=mesh['grp'=4,'mem'=32] {'grp'}, dimensions={0} | all-to-all | bytes 2048 | tf_op jit(solution)/shard_map/all_to_all | solution.py:39
  34.5 0.1 all_to_all.24
  34.5 0.5 broadcast.45
  35.1 0.7 reduce.8
  35.7 0.1 reshape.52
  35.8 25.8 %all-gather = s32[32,1,256]{2,1,0:T(1,128)S(1)} all-gather(s32[1,1,256]{2,1,0:T(1,128)S(1)} %reshape.52), channel_id=1, replica_groups=mesh['grp'=4,'mem'=32] {'mem'}, dimensions={0}, use_global_device_ids=true | all-gather | bytes 33792 | tf_op jit(solution)/shard_map/all_gather | solution.py:44
  61.6 37.4 %all-gather.3.cloned.1.call-done = bf16[8192,1024]{1,0:T(8,128)(2,1)} async-done(((bf16[256,1024]{1,0:T(8,128)(2,1)}), bf16[8192,1024]{1,0:T(8,128)(2,1)}) %all-gather.3.cloned.1.call-update) | async-done | bytes 16777232 | tf_op jit(solution)/shard_map/all_gather | solution.py:41
  99.0 10.6 %fusion = f32[256]{0:T(256)S(1)} fusion(bf16[256,1024]{1,0:T(8,128)(2,1)} %bitcast.18, bf16[8192,1024]{1,0:T(8,128)(2,1)} %all-gather.3.cloned.1.call-done, s32[256]{0:T(256)S(1)} %all_to_all.24, s32[8192]{0:T(1024)S(1)} %bitcast.20), kind=kOutput, calls=%fused_computation.4 | convolution fusion | flops 4301258752 | bytes 17336320 | tf_op jit(solution)/shard_map/dot_general | solution.py:10
  109.7 0.7 max_broadcast_in_dim.14
  110.3 4.2 %all-to-all-start.2 = ((f32[4,64,1]{1,2,0:T(1,128)}), f32[4,64,1]{1,2,0:T(1,128)S(1)}, u32[]{:S(2)}, u32[]{:S(2)}) async-start(f32[4,64,1]{1,2,0:T(1,128)} %bitcast.7), calls=%async_computation.2 | async-start | bytes 4096 | tf_op jit(solution)/shard_map/all_to_all | solution.py:46
  114.6 5.1 %all-to-all-done.2 = f32[4,64,1]{1,2,0:T(1,128)S(1)} async-done(((f32[4,64,1]{1,2,0:T(1,128)}), f32[4,64,1]{1,2,0:T(1,128)S(1)}, u32[]{:S(2)}, u32[]{:S(2)}) %all-to-all-start.2) | async-done | bytes 1056 | tf_op jit(solution)/shard_map/all_to_all | solution.py:46
  119.7 0.5 broadcast.46
  120.2 0.7 reduce.9
  120.9 0.1 all_to_all.29
  121.0 1.8 %gather_fusion = f32[128]{0:T(128)} fusion(f32[256]{0:T(256)S(1)} %all_to_all.29, s32[1024]{0:T(1024)S(1)} %pad_clamp_fusion), kind=kCustom, calls=%fused_computation | custom fusion | bytes 1536 | tf_op jit(solution)/shard_map/gather | solution.py:47
  (3 shorter events, 0.0 us)
Async XLA Ops:
  6.5 92.5 %all-gather.3.cloned.1.call-start = ((), (), s32[]{:S(2)}) async-start(), calls=%async_computation.3 | async-start | bytes 17301504 | tf_op jit(solution)/shard_map/all_gather | solution.py:41
  110.3 9.4 %all-to-all-start.2 = ((f32[4,64,1]{1,2,0:T(1,128)}), f32[4,64,1]{1,2,0:T(1,128)S(1)}, u32[]{:S(2)}, u32[]{:S(2)}) async-start(f32[4,64,1]{1,2,0:T(1,128)} %bitcast.7), calls=%async_computation.2 | async-start | bytes 4096 | tf_op jit(solution)/shard_map/all_to_all | solution.py:46
Sparse Core Ops, SparseCore 0:
  25.8 73.2 all-gather.2
where the time goes:
time: 130 us
  blocking collectives  47.2 us (36%)
  waiting for transfers between devices  42.5 us (33%)
  between operations  13.4 us (10%)
  matrix products  10.6 us (8%)
  other arithmetic  6.62 us (5%)
  local copies, waits for them, and re-layouts  4.9 us (4%)
  starting transfers between devices  4.25 us (3%)
    all_gather x1, waiting for transfers between devices, body(): gram = block_gram(keys, lax.all_gather(keys, 'mem', axis=0, tiled=True))  37.4 us
    all_gather x1, blocking collectives, body(): lax.all_gather(key_rank, 'mem', axis=0, tiled=True)  25.8 us
    all_to_all x1, blocking collectives, body(): lax.all_to_all(outgoing, 'grp', split_axis=0, concat_axis=0, tiled=True)  13.8 us
    dot_general x1, matrix products, block_gram(): lax.dot_general(queries, others, (((1,), (1,)), ((), ())), preferred_elem...  10.6 us
    all_to_all x1, blocking collectives, body(): lax.all_to_all(out_rank, 'grp', split_axis=0, concat_axis=0, tiled=True)  7.61 us
    all_to_all x1, waiting for transfers between devices, body(): home = lax.all_to_all(best, 'grp', split_axis=0, concat_axis=0, tiled=True)  5.12 us
    all_to_all x1, starting transfers between devices, body(): home = lax.all_to_all(best, 'grp', split_axis=0, concat_axis=0, tiled=True)  4.25 us
  transfers between devices with their start and end apart: 2, of which 2 were waited for; matrix products, arithmetic and copies ran while one was open for 2% of the time, Pallas kernels for 0%

commit v1 on v0

--- a/solution.py
+++ b/solution.py
@@ -4,6 +4,11 @@
 from jax.sharding import PartitionSpec as P
 
 absent_rank = 1073741824
+
+
+def gather_by_exchange(x, axis, dim):
+    copies = jnp.concatenate([x] * lax.axis_size(axis), axis=dim)
+    return lax.all_to_all(copies, axis, dim, dim, tiled=True)
 
 
 def block_gram(queries, others):
@@ -41,7 +46,7 @@
     gram = block_gram(keys, lax.all_gather(keys, "mem", axis=0, tiled=True))
     best = jnp.maximum(
         jnp.full((slots,), -1.0, jnp.float32),
-        row_maxima(gram, key_rank, lax.all_gather(key_rank, "mem", axis=0, tiled=True)),
+        row_maxima(gram, key_rank, gather_by_exchange(key_rank, "mem", 0)),
     )
     home = lax.all_to_all(best, "grp", split_axis=0, concat_axis=0, tiled=True)
     return home[slot]

time: 130 us -> 130 us (level)
  waiting for transfers between devices: 42.5 us -> 53.1 us
  blocking collectives: 47.2 us -> 37 us
    all_gather x1 -> x0, blocking collectives: 25.8 us -> none  [body(): lax.all_gather(key_rank, 'mem', axis=0, tiled=True)]
    all_to_all x0 -> x1, blocking collectives: none -> 15.6 us  [gather_by_exchange(): return lax.all_to_all(copies, axis, dim, dim, tiled=True)]
    all_gather x1, waiting for transfers between devices: 37.4 us -> 48 us  [body(): gram = block_gram(keys, lax.all_gather(keys, 'mem', axis=0, tiled=True))]
where the time goes in v1:
time: 130 us
  waiting for transfers between devices  53.1 us (41%)
  blocking collectives  37 us (28%)
  between operations  13.4 us (10%)
  matrix products  10.6 us (8%)
  other arithmetic  6.62 us (5%)
  local copies, waits for them, and re-layouts  4.84 us (4%)
  starting transfers between devices  4.25 us (3%)
    all_gather x1, waiting for transfers between devices, body(): gram = block_gram(keys, lax.all_gather(keys, 'mem', axis=0, tiled=True))  48 us
    all_to_all x1, blocking collectives, gather_by_exchange(): return lax.all_to_all(copies, axis, dim, dim, tiled=True)  15.6 us
    all_to_all x1, blocking collectives, body(): lax.all_to_all(outgoing, 'grp', split_axis=0, concat_axis=0, tiled=True)  13.8 us
    dot_general x1, matrix products, block_gram(): lax.dot_general(queries, others, (((1,), (1,)), ((), ())), preferred_elem...  10.6 us
    all_to_all x1, blocking collectives, body(): lax.all_to_all(out_rank, 'grp', split_axis=0, concat_axis=0, tiled=True)  7.61 us
    all_to_all x1, waiting for transfers between devices, body(): home = lax.all_to_all(best, 'grp', split_axis=0, concat_axis=0, tiled=True)  5.12 us
    all_to_all x1, starting transfers between devices, body(): home = lax.all_to_all(best, 'grp', split_axis=0, concat_axis=0, tiled=True)  4.25 us
  transfers between devices with their start and end apart: 2, of which 2 were waited for; matrix products, arithmetic and copies ran while one was open for 2% of the time, Pallas kernels for 0%

profile of v1, /device:TPU:0, one launch (start us, length us, event | category | flops | bytes accessed | tf_op | source)
XLA Modules:
  0.0 129.9 jit_solution(9420239891254407428)
XLA Ops:
  6.5 0.0 all-gather.2.cloned.1.call-start
  6.5 1.1 fusion.1
  7.6 0.7 fusion.7
  8.4 0.2 reduce_window_sum.11
  8.6 0.8 select_reduce_fusion
  9.4 0.7 fusion.8
  10.1 1.8 %scatter_custom_fusion.1 = bf16[256,1024]{1,0:T(8,128)(2,1)S(1)} fusion(s32[128]{0:T(128)S(1)} %fusion.8, bf16[128,1024]{1,0:T(8,128)(2,1)} %param.3, f32[128]{0:T(128)S(1)} %add_rsqrt_fusion, bf16[]{:T(256)} %constant.4.clone.1), kind=kCustom, calls=%fused_computation.9 | custom fusion | flops 393216 | bytes 786946 | tf_op jit(solution)/shard_map/scatter | solution.py:40
  11.8 13.8 %all_to_all.36 = bf16[4,64,1024]{2,1,0:T(8,128)(2,1)} all-to-all(bf16[4,64,1024]{2,1,0:T(8,128)(2,1)S(1)} %bitcast.20), channel_id=1, replica_groups=mesh['grp'=4,'mem'=32] {'grp'}, dimensions={0} | all-to-all | bytes 1048576 | tf_op jit(solution)/shard_map/all_to_all | solution.py:43
  25.6 0.0 all-gather.2.cloned.1.call-update
  25.7 1.1 scatter_custom_fusion
  26.8 0.1 all_to_all.24
  26.9 7.6 %all_to_all.37 = s32[4,64,1]{1,2,0:T(1,128)S(1)} all-to-all(s32[4,64,1]{1,2,0:T(1,128)S(1)} %bitcast.22), channel_id=1, replica_groups=mesh['grp'=4,'mem'=32] {'grp'}, dimensions={0} | all-to-all | bytes 2048 | tf_op jit(solution)/shard_map/all_to_all | solution.py:44
  34.5 0.5 broadcast.44
  35.0 0.7 reduce.6
  35.6 0.1 concatenate.6
  35.8 15.6 %all_to_all.38 = s32[32,256,1]{1,2,0:T(1,128)S(1)} all-to-all(s32[32,256,1]{1,2,0:T(1,128)S(1)} %concatenate.7), channel_id=1, replica_groups=mesh['grp'=4,'mem'=32] {'mem'}, dimensions={0} | all-to-all | bytes 65536 | tf_op jit(solution)/shard_map/all_to_all | solution.py:11
  51.4 48.0 %all-gather.2.cloned.1.call-done = bf16[8192,1024]{1,0:T(8,128)(2,1)} async-done(((bf16[256,1024]{1,0:T(8,128)(2,1)}), bf16[8192,1024]{1,0:T(8,128)(2,1)}) %all-gather.2.cloned.1.call-update) | async-done | bytes 16777232 | tf_op jit(solution)/shard_map/all_gather | solution.py:46
  99.3 10.6 %fusion = f32[256]{0:T(256)S(1)} fusion(bf16[256,1024]{1,0:T(8,128)(2,1)} %bitcast.19, bf16[8192,1024]{1,0:T(8,128)(2,1)} %all-gather.2.cloned.1.call-done, s32[256]{0:T(256)S(1)} %concatenate.6, s32[8192]{0:T(1024)S(1)} %bitcast.21), kind=kOutput, calls=%fused_computation.4 | convolution fusion | flops 4301258752 | bytes 17336320 | tf_op jit(solution)/shard_map/dot_general | solution.py:15
  110.0 0.7 max_broadcast_in_dim.14
  110.7 4.2 %all-to-all-start.3 = ((f32[4,64,1]{1,2,0:T(1,128)}), f32[4,64,1]{1,2,0:T(1,128)S(1)}, u32[]{:S(2)}, u32[]{:S(2)}) async-start(f32[4,64,1]{1,2,0:T(1,128)} %bitcast.7), calls=%async_computation.3 | async-start | bytes 4096 | tf_op jit(solution)/shard_map/all_to_all | solution.py:51
  114.9 5.1 %all-to-all-done.3 = f32[4,64,1]{1,2,0:T(1,128)S(1)} async-done(((f32[4,64,1]{1,2,0:T(1,128)}), f32[4,64,1]{1,2,0:T(1,128)S(1)}, u32[]{:S(2)}, u32[]{:S(2)}) %all-to-all-start.3) | async-done | bytes 1056 | tf_op jit(solution)/shard_map/all_to_all | solution.py:51
  120.0 0.5 broadcast.45
  120.5 0.7 reduce.7
  121.2 0.1 all_to_all.31
  121.3 1.8 %gather_fusion = f32[128]{0:T(128)} fusion(f32[256]{0:T(256)S(1)} %all_to_all.31, s32[1024]{0:T(1024)S(1)} %pad_clamp_fusion), kind=kCustom, calls=%fused_computation | custom fusion | bytes 1536 | tf_op jit(solution)/shard_map/gather | solution.py:52
  (4 shorter events, 0.0 us)
Async XLA Ops:
  6.5 92.8 %all-gather.2.cloned.1.call-start = ((), (), s32[]{:S(2)}) async-start(), calls=%async_computation.4 | async-start | bytes 17301504 | tf_op jit(solution)/shard_map/all_gather | solution.py:46
  110.7 9.4 %all-to-all-start.3 = ((f32[4,64,1]{1,2,0:T(1,128)}), f32[4,64,1]{1,2,0:T(1,128)S(1)}, u32[]{:S(2)}, u32[]{:S(2)}) async-start(f32[4,64,1]{1,2,0:T(1,128)} %bitcast.7), calls=%async_computation.3 | async-start | bytes 4096 | tf_op jit(solution)/shard_map/all_to_all | solution.py:51
Sparse Core Ops, SparseCore 0:
  25.8 73.5 all-gather.1
